TPU v7x, 256 devices: a whole 4x4x8 slice. The times are simulated.
256 devices in a mesh: cfg: 32 (over y, x, core), tm: 8 (over z).
Axes of the slice: x: 4, y: 4, z: 8, core: 2. Of those that a mesh axis runs over, the one named last changes fastest.
Arguments:
- targets: float32 [8192, 1024], P('cfg', 'tm'), may hold values from -6 to 6
- features: float32 [8192, 64], P('cfg'), may hold values from -6 to 6
- inv_scales: float32 [64], replicated, may hold values from 0.05 to 0.3
- noise: float32 [8192], P('cfg'), may hold values from 0.1 to 1
- time_kernel: float32 [1024, 1024], P('tm'), may hold values from -1 to 1, as said below
- block_mask: int32 [8192, 8], P('cfg', 'tm'), may hold values from 0 to 1, as said below
Outputs:
- solution_field: float32 [8192, 1024], P('cfg', 'tm')
- residual: float32 [8192, 1024], P('cfg', 'tm')
Inputs may be any that keep to these rules, and one draw needn't show every extreme that they name: `block_mask`: each configuration observes one contiguous run of blocks that starts at a block of 0 to 2 and has at least one block; some runs start late and some reach the last block. `time_kernel`: symmetric positive definite, with unit diagonal.
All inputs are finite; a program needn't handle non-finite values.
Results may differ from a plain program's by a relative error of at most 0.00026.
Values sent between devices are 32-bit elements; how exact they have to be, the bound alone decides.
A program may use at most 64 MiB of HBM per device.

v0:
```python
import jax
import jax.numpy as jnp
from jax import lax
from jax.sharding import PartitionSpec as P

BLOCK = 128
ITERS = 2


def matern(left, right):
    cross = jnp.dot(
        left, right.T, precision=lax.Precision.HIGHEST, preferred_element_type=jnp.float32
    )
    dist2 = (
        jnp.sum(left * left, axis=1)[:, None]
        + jnp.sum(right * right, axis=1)[None, :]
        - 2.0 * cross
    )
    scaled_dist = jnp.sqrt(3.0) * jnp.sqrt(jnp.maximum(dist2, 0.0))
    return (1.0 + scaled_dist) * jnp.exp(-scaled_dist)


def body(targets, features, inv_scales, noise, time_kernel, block_mask):
    mask = jnp.repeat(block_mask.astype(jnp.float32), BLOCK, axis=1)
    scaled = features * inv_scales[None, :]
    every = lax.all_gather(scaled, "cfg", axis=0, tiled=True)
    tile = matern(scaled, every)
    residual = mask * targets
    direction = residual
    solution_field = jnp.zeros_like(residual)
    norm_now = lax.psum(jnp.sum(residual * residual), ("cfg", "tm"))
    for step in range(ITERS):
        operate_mixed = jnp.dot(
            tile,
            lax.all_gather(mask * direction, "cfg", axis=0, tiled=True),
            precision=lax.Precision.HIGHEST,
            preferred_element_type=jnp.float32,
        )
        image = (
            mask
            * lax.psum_scatter(
                jnp.dot(
                    time_kernel.T,
                    operate_mixed.T,
                    precision=lax.Precision.HIGHEST,
                    preferred_element_type=jnp.float32,
                ),
                "tm",
                scatter_dimension=0,
                tiled=True,
            ).T
            + noise[:, None] * direction
        )
        curv = lax.psum(jnp.sum(direction * image), ("cfg", "tm"))
        alpha = norm_now / curv
        solution_field = solution_field + alpha * direction
        residual = residual - alpha * image
        norm_next = lax.psum(jnp.sum(residual * residual), ("cfg", "tm"))
        direction = residual + norm_next / norm_now * direction
        norm_now = norm_next
    return (solution_field, residual)


def solution(mesh):
    return jax.shard_map(
        body,
        mesh=mesh,
        in_specs=(P("cfg", "tm"), P("cfg", None), P(), P("cfg"), P("tm", None), P("cfg", "tm")),
        out_specs=(P("cfg", "tm"), P("cfg", "tm")),
        check_vma=False,
    )
```

profile of v0, /device:TPU:1, one launch (start us, length us, event | category | flops | bytes accessed | tf_op | source)
XLA Modules:
  0.0 509.3 jit_solution(8296447586257143950)
XLA Ops:
  7.2 0.0 copy-start
  7.2 0.0 all-gather.4.cloned.1.call-start
  7.2 1.6 multiply_reduce_fusion.5
  8.8 0.0 all-gather.4.cloned.1.call-update
  8.8 0.0 all-gather.6.cloned.1.call-start
  8.9 0.7 convert_element_type.5
  9.6 1.7 multiply_multiply_fusion
  11.2 0.0 all-gather.6.cloned.1.call-update
  11.3 0.0 reduce-scatter.3.cloned.1.call-start
  11.3 53.5 %all-gather.4.cloned.1.call-done = f32[8192,64]{0,1:T(8,128)} async-done(((f32[256,64]{0,1:T(8,128)}), f32[8192,64]{0,1:T(8,128)}) %all-gather.4.cloned.1.call-update) | async-done | bytes 2097168 | tf_op jit(solution)/shard_map/all_gather | solution.py:26
  64.8 1.8 multiply_reduce_fusion
  66.6 14.5 %exponential_multiply_fusion = f32[256,8192]{1,0:T(8,128)} fusion(f32[256,64]{0,1:T(8,128)} %get-tuple-element.7, f32[8192,64]{0,1:T(8,128)} %all-gather.4.cloned.1.call-done, f32[8192]{0:T(1024)S(1)} %multiply_reduce_fusion, f32[256]{0:T(256)S(1)} %get-tuple-element.6), kind=kOutput, calls=%fused_computation.5 | convolution fusion | flops 1627389952 | bytes 10585088 | tf_op jit(solution)/shard_map/dot_general | solution.py:11
  81.0 0.0 copy-start.1
  81.0 0.0 copy-start.3
  81.0 37.4 %all-gather.6.cloned.1.call-done = f32[8192,128]{1,0:T(8,128)} async-done(((f32[256,128]{1,0:T(8,128)}), f32[8192,128]{1,0:T(8,128)}) %all-gather.6.cloned.1.call-update) | async-done | bytes 4194320 | tf_op jit(solution)/shard_map/all_gather | solution.py:35
  118.5 9.8 %fusion.4 = f32[256,128]{1,0:T(8,128)S(1)} fusion(f32[256,8192]{1,0:T(8,128)} %exponential_multiply_fusion, f32[8192,128]{1,0:T(8,128)} %all-gather.6.cloned.1.call-done), kind=kOutput, calls=%fused_computation.23 | convolution fusion | flops 3221225472 | bytes 12713984 | tf_op jit(solution)/shard_map/dot_general | solution.py:33
  128.3 0.0 copy-done
  128.3 2.0 convolution_bitcast_fusion.1
  130.3 0.0 reduce-scatter.3.cloned.1.call-update
  130.4 0.0 all-gather.8.cloned.1.call-start
  130.4 33.7 %reduce-scatter.3.cloned.1.call-done = f32[128,256]{0,1:T(8,128)} async-done(((f32[1024,256]{0,1:T(8,128)}), f32[128,256]{0,1:T(8,128)}) %reduce-scatter.3.cloned.1.call-update) | async-done | bytes 131088 | tf_op jit(solution)/shard_map/reduce_scatter | solution.py:41
  164.1 0.0 copy-done.1
  164.1 0.0 copy-done.3
  164.1 0.0 copy-start.2
  164.1 1.8 multiply_reduce_fusion.3
  165.8 79.3 %all-reduce = (f32[]{:T(128)}, f32[]{:T(128)}) all-reduce(f32[]{:T(128)} %get-tuple-element.3, f32[]{:T(128)} %get-tuple-element.2), channel_id=1, replica_groups=mesh['cfg'=32,'tm'=8] {'cfg','tm'}, use_global_device_ids=true, to_apply=%region_1.0 | all-reduce | flops 2 | bytes 16 | tf_op jit(solution)/shard_map/psum | solution.py:31
  246.5 1.7 multiply_reduce_fusion.2
  248.2 73.5 %psum.30 = f32[]{:T(128)} all-reduce(f32[]{:T(128)} %multiply_reduce_fusion.2), channel_id=1, replica_groups=mesh['cfg'=32,'tm'=8] {'cfg','tm'}, use_global_device_ids=true, to_apply=%region_8.0 | all-reduce | flops 1 | bytes 8 | tf_op jit(solution)/shard_map/psum | solution.py:58
  323.0 1.7 broadcast_multiply_fusion
  324.8 0.0 all-gather.8.cloned.1.call-update
  324.8 0.0 reduce-scatter.5.cloned.1.call-start
  324.9 48.3 %all-gather.8.cloned.1.call-done = f32[8192,128]{1,0:T(8,128)} async-done(((f32[256,128]{1,0:T(8,128)}), f32[8192,128]{1,0:T(8,128)}) %all-gather.8.cloned.1.call-update) | async-done | bytes 4194320 | tf_op jit(solution)/shard_map/all_gather | solution.py:35
  373.2 9.8 %fusion.5 = f32[256,128]{1,0:T(8,128)S(1)} fusion(f32[256,8192]{1,0:T(8,128)} %exponential_multiply_fusion, f32[8192,128]{1,0:T(8,128)} %all-gather.8.cloned.1.call-done), kind=kOutput, calls=%fused_computation.24 | convolution fusion | flops 3221225472 | bytes 12713984 | tf_op jit(solution)/shard_map/dot_general | solution.py:33
  383.0 2.0 convolution_bitcast_fusion
  384.9 0.0 reduce-scatter.5.cloned.1.call-update
  385.0 33.1 %reduce-scatter.5.cloned.1.call-done = f32[128,256]{0,1:T(8,128)} async-done(((f32[1024,256]{0,1:T(8,128)}), f32[128,256]{0,1:T(8,128)}) %reduce-scatter.5.cloned.1.call-update) | async-done | bytes 131088 | tf_op jit(solution)/shard_map/reduce_scatter | solution.py:41
  418.1 0.0 copy-done.2
  418.1 1.7 multiply_reduce_fusion.1
  419.7 79.9 %psum.31 = f32[]{:T(128)} all-reduce(f32[]{:T(128)} %multiply_reduce_fusion.1), channel_id=1, replica_groups=mesh['cfg'=32,'tm'=8] {'cfg','tm'}, use_global_device_ids=true, to_apply=%region_11.0 | all-reduce | flops 1 | bytes 8 | tf_op jit(solution)/shard_map/psum | solution.py:54
  501.0 1.8 multiply_subtract_fusion
Async XLA Ops:
  7.2 121.1 %copy-start = (f32[128,1024]{1,0:T(8,128)S(1)}, f32[128,1024]{1,0:T(8,128)}, u32[]{:S(2)}) copy-start(f32[128,1024]{1,0:T(8,128)} %param.10) | copy-start | bytes 1572868
  7.2 57.6 %all-gather.4.cloned.1.call-start = ((), (), s32[]{:S(2)}) async-start(), calls=%async_computation.2 | async-start | bytes 2162688 | tf_op jit(solution)/shard_map/all_gather | solution.py:26
  8.8 109.6 %all-gather.6.cloned.1.call-start = ((), (), s32[]{:S(2)}) async-start(), calls=%async_computation.3 | async-start | bytes 4325376 | tf_op jit(solution)/shard_map/all_gather | solution.py:35
  11.3 152.8 %reduce-scatter.3.cloned.1.call-start = ((), (), s32[]{:S(2)}) async-start(), calls=%async_computation.4 | async-start | bytes 1179648 | tf_op jit(solution)/shard_map/reduce_scatter | solution.py:41
  81.0 83.0 %copy-start.1 = (f32[256,128]{1,0:T(8,128)S(1)}, f32[256,128]{1,0:T(8,128)}, u32[]{:S(2)}) copy-start(f32[256,128]{1,0:T(8,128)} %param.6) | copy-start | bytes 393220
  81.0 83.0 %copy-start.3 = (f32[256]{0:T(256)S(1)}, f32[256]{0:T(256)}, u32[]{:S(2)}) copy-start(f32[256]{0:T(256)} %param.9) | copy-start | bytes 3076
  130.4 242.8 %all-gather.8.cloned.1.call-start = ((), (), s32[]{:S(2)}) async-start(), calls=%async_computation.5 | async-start | bytes 4325376 | tf_op jit(solution)/shard_map/all_gather | solution.py:35
  164.1 254.0 %copy-start.2 = (f32[128,256]{0,1:T(8,128)S(1)}, f32[128,256]{0,1:T(8,128)}, u32[]{:S(2)}) copy-start(f32[128,256]{0,1:T(8,128)} %reduce-scatter.3.cloned.1.call-done) | copy-start | bytes 393220
  324.8 93.2 %reduce-scatter.5.cloned.1.call-start = ((), (), s32[]{:S(2)}) async-start(), calls=%async_computation.6 | async-start | bytes 1179648 | tf_op jit(solution)/shard_map/reduce_scatter | solution.py:41
Sparse Core Ops, SparseCore 0:
  11.0 53.7 all-gather.3
  67.9 50.5 all-gather.5
  130.5 33.5 reduce-scatter.2
  324.9 48.1 all-gather.7
  385.1 32.9 reduce-scatter.4
where the time goes:
time: 510 us; the launch traced here: 509 us
  blocking collectives  233 us (46%)
  waiting for transfers between devices  206 us (40%)
  matrix products  38.1 us (7%)
  between operations  17.8 us (3%)
  other arithmetic  14.4 us (3%)
    all_gather x2, waiting for transfers between devices, body(): lax.all_gather(mask * direction, 'cfg', axis=0, tiled=True)  85.7 us
    psum x1, blocking collectives, body(): curv = lax.psum(jnp.sum(direction * image), ('cfg', 'tm'))  79.9 us
    psum x1, blocking collectives, body(): norm_now = lax.psum(jnp.sum(residual * residual), ('cfg', 'tm'))  79.3 us
    psum x1, blocking collectives, body(): norm_next = lax.psum(jnp.sum(residual * residual), ('cfg', 'tm'))  73.5 us
    reduce_scatter x2, waiting for transfers between devices, body(): lax.psum_scatter(jnp.dot(time_kernel.T, operate_mixed.T, precision=lax.Pr...  66.7 us
    all_gather x1, waiting for transfers between devices, body(): every = lax.all_gather(scaled, 'cfg', axis=0, tiled=True)  53.5 us
    dot_general x2, matrix products, body(): jnp.dot(tile, lax.all_gather(mask * direction, 'cfg', axis=0, tiled=True)...  19.6 us
    dot_general x1, matrix products, matern(): jnp.dot(left, right.T, precision=lax.Precision.HIGHEST, preferred_element...  14.5 us
  transfers between devices with their start and end apart: 5, of which 5 were waited for; matrix products, arithmetic and copies ran while one was open for 4% of the time, Pallas kernels for 0%

commit v1 on v0

v1 whole, which is shorter than its diff:
```python
import math

import jax
import jax.numpy as jnp
from jax import lax
from jax.experimental import pallas as pl
from jax.experimental.pallas import tpu as pltpu
from jax.sharding import PartitionSpec as P

MESH = pl.DeviceIdType.MESH
F32, BF16 = jnp.float32, jnp.bfloat16
NY, NX, NCORE, NZ = 4, 4, 2, 8
PLANE = NY * NX * NCORE
ROWS, COLS, FEAT = 256, 128, 64
DEPTH = 384
CHUNKS = 4
NSEM = 192
UNIT = math.sqrt(3.0) * math.log2(math.e)
LN2 = math.log(2.0)


def split2(x):
    hi = x.astype(BF16)
    return hi, (x - hi.astype(F32)).astype(BF16)


def nt_dot(a, b):
    return lax.dot_general(a, b, (((1,), (1,)), ((), ())), preferred_element_type=F32)


def kernel(
    tgt, feat, isc, noise_ref, tk, bm, sol, res,
    zg, wy, fy, fx, fl, fr, kc, wb, vb, tn, p, rel, fin, nz, mk,
    arsrc, arp, arz, ss, rs, ars, arr,
):
    me, z = lax.axis_index("cfg"), lax.axis_index("tm")
    core = lax.rem(me, NCORE)
    x = lax.rem(me // NCORE, NX)
    y = me // (NCORE * NX)

    def at(yy, xx, cc):
        return ((yy * NX + xx) * NCORE + cc, z)

    right, left = at(y, lax.rem(x + 1, NX), core), at(y, lax.rem(x + NX - 1, NX), core)
    up, down = at(lax.rem(y + 1, NY), x, core), at(lax.rem(y + NY - 1, NY), x, core)
    mate = at(y, x, 1 - core)
    zup, zdown = (me, lax.rem(z + 1, NZ)), (me, lax.rem(z + NZ - 1, NZ))
    plane = [(lax.rem(me + r, PLANE), z) for r in range(1, PLANE)]
    column = [(me, lax.rem(z + r, NZ)) for r in range(1, NZ)]

    copies = []

    def copy(src, dst, dev):
        i = len(copies)
        assert i < NSEM
        d = pltpu.make_async_remote_copy(
            src_ref=src, dst_ref=dst, send_sem=ss.at[i], recv_sem=rs.at[i],
            device_id=dev, device_id_type=MESH,
        )
        copies.append(d)
        return d

    barrier = pltpu.get_barrier_semaphore()
    for dev in plane + column:
        pl.semaphore_signal(barrier, inc=1, device_id=dev, device_id_type=MESH)

    mk[...] = jnp.broadcast_to(bm[...].astype(F32), (COLS, ROWS)).T
    nz[...] = jnp.broadcast_to(noise_ref[...], (COLS, ROWS)).T
    zg[0, 0] = mk[...] * tgt[...]
    fscaled = feat[...] * (isc[...].T * UNIT)
    fy[0, 0] = fscaled
    fx[0] = fscaled

    pl.semaphore_wait(barrier, len(plane) + len(column))

    def ring4(buf, nh, fwd, back):
        d = {}
        for h in range(nh):
            d["R1", h] = copy(buf(0, h), buf(1, h), fwd)
            d["L1", h] = copy(buf(0, h), buf(3, h), back)
        for h in range(nh):
            if h < nh // 2:
                d["2", h] = copy(buf(1, h), buf(2, h), fwd)
            else:
                d["2", h] = copy(buf(3, h), buf(2, h), back)
        return d

    def y_ring(buf, nh):
        d = ring4(lambda k, h: buf(0, k, h), nh, up, down)
        for k in (0, 1, 3, 2):
            for h in range(nh):
                d["m", k, h] = copy(buf(0, k, h), buf(1, k, h), mate)
        return d

    def ring_step1(d, nh, mated):
        for h in range(nh):
            d["R1", h].wait_recv()
            if h < nh // 2:
                d["2", h].start()
            if mated:
                d["m", 1, h].start()
            d["L1", h].wait_recv()
            if h >= nh // 2:
                d["2", h].start()
            if mated:
                d["m", 3, h].start()

    def ring_step2(d, nh, mated):
        for h in range(nh):
            d["2", h].wait_recv()
            if mated:
                d["m", 2, h].start()

    def mate_wait(d, nh, k):
        for h in range(nh):
            d["m", k, h].wait_recv()

    CR = ROWS // CHUNKS

    def z_ring(it):
        d = {}
        for s in range(1, 5):
            for c in range(CHUNKS):
                sl = pl.ds(c * CR, CR)
                if s < 4 or c < CHUNKS // 2:
                    d["R", s, c] = copy(zg.at[it, s - 1, sl], zg.at[it, s, sl], zup)
                if s < 4 or c >= CHUNKS // 2:
                    d["L", s, c] = copy(zg.at[it, (9 - s) % 8, sl], zg.at[it, 8 - s, sl], zdown)
        return d

    def z_start(d, c):
        d["R", 1, c].start()
        d["L", 1, c].start()

    def z_step(d, s):
        for c in range(CHUNKS):
            for way in "RL":
                if (way, s, c) in d:
                    d[way, s, c].wait_recv()
                if (way, s + 1, c) in d:
                    d[way, s + 1, c].start()

    def plane_copies(n):
        return [
            pltpu.make_async_remote_copy(
                src_ref=arsrc.at[n, 0], dst_ref=arp.at[n, r], send_sem=ars.at[n, 0], recv_sem=arr.at[n, 0],
                device_id=dev, device_id_type=MESH,
            )
            for r, dev in enumerate(plane)
        ]

    def column_copies(n):
        return [
            pltpu.make_async_remote_copy(
                src_ref=arsrc.at[n, 1], dst_ref=arz.at[n, r], send_sem=ars.at[n, 1], recv_sem=arr.at[n, 1],
                device_id=dev, device_id_type=MESH,
            )
            for r, dev in enumerate(column)
        ]

    def whole(n, j):
        buf, dev = (arp, plane[0]) if j == 0 else (arz, column[0])
        return pltpu.make_async_remote_copy(
            src_ref=buf.at[n], dst_ref=buf.at[n], send_sem=ars.at[n, j], recv_sem=arr.at[n, j],
            device_id=dev, device_id_type=MESH,
        )

    def sum_start(n, first, second):
        arsrc[n, 0, 0:1] = jnp.sum(first, axis=0, keepdims=True)
        arsrc[n, 0, 1:2] = jnp.sum(second, axis=0, keepdims=True)
        for d in plane_copies(n):
            d.start()

    def sum_middle(n):
        whole(n, 0).wait_recv()
        arsrc[n, 1] = arsrc[n, 0] + jnp.sum(arp[n], axis=0)
        for d in column_copies(n):
            d.start()

    def sum_end(n):
        whole(n, 1).wait_recv()
        both = arsrc[n, 1] + jnp.sum(arz[n], axis=0)
        both = jnp.sum(both, axis=1, keepdims=True)
        return both[0:1], both[1:2]

    dz = z_ring(0)
    for c in range(CHUNKS):
        z_start(dz, c)
    FH = ROWS // 2
    dfx = ring4(lambda k, h: fx.at[k, :, pl.ds(h * FH, FH)], 2, right, left)
    dfy = y_ring(lambda c, k, h: fy.at[c, k, :, pl.ds(h * FH, FH)], 2)
    for h in range(2):
        for way in ("R1", "L1"):
            dfy[way, h].start()
            dfx[way, h].start()
        dfy["m", 0, h].start()

    for k in range(NZ):
        o = lax.rem(z + NZ - k, NZ)
        hi, lo = split2(tk[:, pl.ds(pl.multiple_of(o * COLS, COLS), COLS)])
        tn[0:COLS, k * COLS : (k + 1) * COLS] = hi
        tn[COLS : 2 * COLS, k * COLS : (k + 1) * COLS] = lo

    def parts(block):
        hi = block.astype(BF16).astype(F32)
        lo = (block - hi).astype(BF16).astype(F32)
        kept = hi + lo
        n = jnp.sum(kept * kept, axis=0, keepdims=True)
        n1 = n.astype(BF16).astype(F32)
        n2 = (n - n1).astype(BF16).astype(F32)
        return hi, lo, jnp.concatenate([n1, n2, n - n1 - n2], axis=0)

    pad = DEPTH - 4 * FEAT
    row = lax.broadcasted_iota(jnp.int32, (pad, ROWS), 0)

    def place(n, first):
        out = jnp.where((row >= 3 - first) & (row < 6 - first), 1.0, 0.0)
        for i in range(3):
            out = jnp.where(row == first + i, jnp.broadcast_to(n[i : i + 1], (pad, ROWS)), out)
        return out

    def build_left(k):
        hi, lo, n = parts(fx[k])
        stack = jnp.concatenate([-2.0 * hi, -2.0 * hi, -2.0 * lo, -2.0 * lo, place(n, 0)], axis=0)
        fl[k * ROWS : (k + 1) * ROWS, :] = stack.T.astype(BF16)

    def build_right(c, k):
        hi, lo, n = parts(fy[c, k])
        stack = jnp.concatenate([hi, lo, hi, lo, place(n, 3)], axis=0)
        j = c * NY + k
        fr[:, j * ROWS : (j + 1) * ROWS] = stack.astype(BF16)

    def make_kernel(c, k):
        build_right(c, k)
        j = c * NY + k
        cols = slice(j * ROWS, (j + 1) * ROWS)
        low = slice((8 + j) * ROWS, (9 + j) * ROWS)

        def one(i, carry):
            sl = pl.ds(pl.multiple_of(i * ROWS, ROWS), ROWS)
            d2 = jnp.dot(fl[sl, :], fr[:, cols], preferred_element_type=F32)
            d2 = jnp.maximum(d2, 1e-30)
            u = d2 * lax.rsqrt(d2)
            value = (1.0 + LN2 * u) * jnp.exp2(-u)
            hi, lo = split2(value)
            kc[sl, cols] = hi
            kc[sl, low] = lo
            return carry

        lax.fori_loop(0, NX, one, 0)

    def split_field(k, block):
        hi, lo = split2(block)
        vb[:, k * COLS : (k + 1) * COLS] = hi
        vb[:, (NZ + k) * COLS : (NZ + k + 1) * COLS] = lo

    def timed(c):
        sl = slice(c * ROWS // 2, (c + 1) * ROWS // 2)
        half = NZ * COLS
        acc = nt_dot(vb[sl, :half], tn[...]) + nt_dot(vb[sl, half:], tn[...])
        return acc[:, :COLS] + acc[:, COLS:]

    def split_w(it, c, k):
        hi, lo = split2(wy[it, c, k])
        j = c * NY + k
        wb[j * ROWS : (j + 1) * ROWS, :COLS] = hi
        wb[j * ROWS : (j + 1) * ROWS, COLS:] = lo

    def apply_rows(it, k):
        half = 8 * ROWS
        sl = slice(k * ROWS, (k + 1) * ROWS)
        acc = jnp.dot(kc[sl, :half], wb[...], preferred_element_type=F32)
        acc += jnp.dot(kc[sl, half:], wb[...], preferred_element_type=F32)
        p[it, k] = acc[:, :COLS] + acc[:, COLS:]

    HR = ROWS // 2
    A, B = pl.ds(0, HR), pl.ds(HR, HR)

    def spread(it):
        relay_r = copy(p.at[it, 2, A], rel.at[it, 0], right)
        relay_l = copy(p.at[it, 2, B], rel.at[it, 1], left)
        own_r = copy(p.at[it, 3, B], fin.at[it, 0, B], right)
        own_l = copy(p.at[it, 1, A], fin.at[it, 1, A], left)
        sum_r = copy(p.at[it, 3, A], fin.at[it, 0, A], right)
        sum_l = copy(p.at[it, 1, B], fin.at[it, 1, B], left)
        apply_rows(it, 2)
        relay_r.start()
        relay_l.start()
        apply_rows(it, 3)
        own_r.start()
        apply_rows(it, 1)
        own_l.start()
        relay_r.wait_recv()
        p[it, 3, A] += rel[it, 0]
        sum_r.start()
        relay_l.wait_recv()
        p[it, 1, B] += rel[it, 1]
        sum_l.start()
        apply_rows(it, 0)
        own_r.wait_recv()
        own_l.wait_recv()
        sum_r.wait_recv()
        sum_l.wait_recv()
        return p[it, 0] + fin[it, 0] + fin[it, 1]

    split_field(0, zg[0, 0])
    ring_step1(dfx, 2, False)
    ring_step1(dfy, 2, True)
    build_left(0)
    z_step(dz, 1)
    ring_step2(dfx, 2, False)
    ring_step2(dfy, 2, True)
    for k in (1, 3, 2):
        build_left(k)
    split_field(1, zg[0, 1])
    split_field(7, zg[0, 7])
    make_kernel(0, 0)
    make_kernel(0, 1)
    z_step(dz, 2)
    split_field(2, zg[0, 2])
    split_field(6, zg[0, 6])
    make_kernel(0, 3)
    make_kernel(0, 2)
    z_step(dz, 3)
    split_field(3, zg[0, 3])
    split_field(5, zg[0, 5])
    mate_wait(dfy, 2, 0)
    make_kernel(1, 0)
    mate_wait(dfy, 2, 1)
    make_kernel(1, 1)
    z_step(dz, 4)
    split_field(4, zg[0, 4])

    def send_w(it):
        d = y_ring(lambda c, k, h: wy.at[it, c, k, pl.ds(h * HR, HR)], 2)
        for h in range(2):
            wy[it, 0, 0, h * HR : (h + 1) * HR] = timed(h)
            d["R1", h].start()
            d["L1", h].start()
            d["m", 0, h].start()
        return d

    dw = send_w(0)
    mate_wait(dfy, 2, 3)
    make_kernel(1, 3)
    ring_step1(dw, 2, True)
    mate_wait(dfy, 2, 2)
    make_kernel(1, 2)

    def finish_w(it, d, stepped):
        split_w(it, 0, 0)
        if not stepped:
            ring_step1(d, 2, True)
        split_w(it, 0, 1)
        split_w(it, 0, 3)
        mate_wait(d, 2, 0)
        split_w(it, 1, 0)
        ring_step2(d, 2, True)
        split_w(it, 0, 2)
        for k in (1, 3, 2):
            mate_wait(d, 2, k)
            split_w(it, 1, k)

    finish_w(0, dw, True)
    total = spread(0)
    r0 = zg[0, 0]
    q = mk[...] * total + nz[...] * r0
    zg[1, 0] = q

    dz = z_ring(1)
    for c in range(CHUNKS):
        z_start(dz, c)
    sum_start(0, r0 * r0, r0 * q)
    z_step(dz, 1)
    sum_middle(0)
    z_step(dz, 2)
    norm0, curv0 = sum_end(0)
    alpha = norm0 / curv0

    def residual_block(k):
        return zg[0, k] - alpha * zg[1, k]

    r1 = residual_block(0)
    res[...] = r1
    sum_start(1, r1 * r1, r1)
    split_field(0, r1)
    for k in (1, 7, 2, 6):
        split_field(k, residual_block(k))
    z_step(dz, 3)
    for k in (3, 5):
        split_field(k, residual_block(k))
    sum_middle(1)
    z_step(dz, 4)
    split_field(4, residual_block(4))
    dw = send_w(1)
    norm1, _ = sum_end(1)
    finish_w(1, dw, False)
    total = spread(1)

    beta = norm1 / norm0
    r1 = res[...]
    d1 = r1 + beta * zg[0, 0]
    image = mk[...] * total + nz[...] * r1 + beta * zg[1, 0]
    sum_start(2, d1 * image, d1)
    p[1, 0] = d1
    p[0, 0] = image
    sum_middle(2)
    curv1, _ = sum_end(2)
    alpha1 = norm1 / curv1
    sol[...] = alpha * zg[0, 0] + alpha1 * p[1, 0]
    res[...] = res[...] - alpha1 * p[0, 0]

    for d in copies:
        d.wait_send()
    for n in range(3):
        whole(n, 0).wait_send()
        whole(n, 1).wait_send()


def body(targets, features, inv_scales, noise, time_kernel, block_mask):
    vmem = pl.BlockSpec(memory_space=pltpu.VMEM)
    block = jax.ShapeDtypeStruct((ROWS, COLS), F32)
    return pl.pallas_call(
        kernel,
        out_shape=(block, block),
        in_specs=[vmem] * 6,
        out_specs=(vmem, vmem),
        scratch_shapes=[
            pltpu.VMEM((2, NZ, ROWS, COLS), F32),
            pltpu.VMEM((2, NCORE, NY, ROWS, COLS), F32),
            pltpu.VMEM((NCORE, NY, FEAT, ROWS), F32),
            pltpu.VMEM((NX, FEAT, ROWS), F32),
            pltpu.VMEM((NX * ROWS, DEPTH), BF16),
            pltpu.VMEM((DEPTH, 8 * ROWS), BF16),
            pltpu.VMEM((NX * ROWS, 16 * ROWS), BF16),
            pltpu.VMEM((8 * ROWS, 2 * COLS), BF16),
            pltpu.VMEM((ROWS, 2 * NZ * COLS), BF16),
            pltpu.VMEM((2 * COLS, NZ * COLS), BF16),
            pltpu.VMEM((2, NX, ROWS, COLS), F32),
            pltpu.VMEM((2, 2, ROWS // 2, COLS), F32),
            pltpu.VMEM((2, 2, ROWS, COLS), F32),
            pltpu.VMEM((ROWS, COLS), F32),
            pltpu.VMEM((ROWS, COLS), F32),
            pltpu.VMEM((3, 2, 2, COLS), F32),
            pltpu.VMEM((3, PLANE - 1, 2, COLS), F32),
            pltpu.VMEM((3, NZ - 1, 2, COLS), F32),
            pltpu.SemaphoreType.DMA((NSEM,)),
            pltpu.SemaphoreType.DMA((NSEM,)),
            pltpu.SemaphoreType.DMA((3, 2)),
            pltpu.SemaphoreType.DMA((3, 2)),
        ],
        compiler_params=pltpu.CompilerParams(
            collective_id=0, has_side_effects=True, vmem_limit_bytes=40 * 1024 * 1024
        ),
    )(
        targets, features.T, inv_scales.reshape(1, FEAT), noise.reshape(1, ROWS), time_kernel, block_mask.T
    )


def solution(mesh):
    return jax.shard_map(
        body,
        mesh=mesh,
        in_specs=(P("cfg", "tm"), P("cfg", None), P(), P("cfg"), P("tm", None), P("cfg", "tm")),
        out_specs=(P("cfg", "tm"), P("cfg", "tm")),
        check_vma=False,
    )
```

time: 510 us -> 102 us (0.20)
  blocking collectives: 233 us -> 0 us
  waiting for transfers between devices: 206 us -> 0 us
  Pallas kernels: 0 us -> 96.2 us
  matrix products: 38.1 us -> 0 us
  between operations: 17.8 us -> 0.67 us
  other arithmetic: 14.4 us -> 0 us
    psum x3 -> x0, blocking collectives: 233 us -> none  [the longest x1 79.9 us: body(): curv = lax.psum(jnp.sum(direction * image), ('cfg', 'tm'))]
    all_gather x3 -> x0, waiting for transfers between devices: 139 us -> none  [the longest x2 85.7 us: body(): lax.all_gather(mask * direction, 'cfg', axis=0, tiled=True)]
    pallas_call x0 -> x1, Pallas kernels: none -> 96.2 us  [body(): pl.pallas_call(kernel, out_shape=(block, block), in_specs=[vmem] * 6, out...]
    reduce_scatter x2 -> x0, waiting for transfers between devices: 66.7 us -> none  [body(): lax.psum_scatter(jnp.dot(time_kernel.T, operate_mixed.T, precision=lax.Pr...]
    dot_general x5 -> x0, matrix products: 38.1 us -> none  [the longest x2 19.6 us: body(): jnp.dot(tile, lax.all_gather(mask * direction, 'cfg', axis=0, tiled=True)...]
    reduce_sum x5 -> x0, other arithmetic: 8.51 us -> none  [the longest x2 3.44 us: body(): curv = lax.psum(jnp.sum(direction * image), ('cfg', 'tm'))]
  transfers between devices with their start and end apart: 5 -> 0, of which waited for: 5 -> 0; matrix products, arithmetic and copies ran while one was open for 4% -> 0% of each run, Pallas kernels for 0% -> 0%
where the time goes in v1:
time: 102 us
  Pallas kernels  96.2 us (94%)
  local copies, waits for them, and re-layouts  4.77 us (5%)
    pallas_call x1, Pallas kernels, body(): pl.pallas_call(kernel, out_shape=(block, block), in_specs=[vmem] * 6, out...  96.2 us
    unnamed x14, local copies, waits for them, and re-layouts  4.77 us

profile of v1, /device:TPU:1, one launch (start us, length us, event | category | flops | bytes accessed | tf_op | source)
XLA Modules:
  0.0 101.7 jit_solution(14544468813743956089)
XLA Ops:
  0.6 0.0 copy-start.4
  0.6 0.0 copy-start.3
  0.7 0.0 copy-start.5
  0.7 0.7 copy-done.4
  1.3 0.0 copy-done.3
  1.3 0.0 copy-done.5
  1.3 0.0 copy-start
  1.3 1.0 %copy-done = f32[128,1024]{1,0:T(8,128)S(1)} copy-done((f32[128,1024]{1,0:T(8,128)S(1)}, f32[128,1024]{1,0:T(8,128)}, u32[]{:S(2)}) %copy-start) | copy-done | bytes 524312
  2.4 0.0 copy-start.1
  2.4 0.9 copy-done.1
  3.3 0.0 copy-start.2
  3.3 0.8 copy-done.2
  4.1 96.2 %shard_map.77 = (f32[256,128]{1,0:T(8,128)S(1)}, f32[256,128]{1,0:T(8,128)S(1)}) custom-call(f32[256,128]{1,0:T(8,128)S(1)} %copy-done.1, f32[64,256]{1,0:T(8,128)S(1)} %bitcast.4, f32[1,64]{1,0:T(1,128)S(1)} %bitcast.7, f32[1,256]{1,0:T(1,128)S(1)} %bitcast.5, f32[128,1024]{1,0:T(8,128)S(1)} %copy-done, s32[1,256]{1,0:T(1,128)S(1)} %bitcast.6), custom_call_target="tpu_custom_call" | custom-call | tf_op jit(solution)/shard_map/pallas_call | solution.py:423
  100.4 0.7 copy.10
  101.0 0.7 copy.11
Async XLA Ops:
  0.6 0.7 copy-start.4
  0.6 0.7 copy-start.3
  0.7 0.7 copy-start.5
  1.3 1.0 %copy-start = (f32[128,1024]{1,0:T(8,128)S(1)}, f32[128,1024]{1,0:T(8,128)}, u32[]{:S(2)}) copy-start(f32[128,1024]{1,0:T(8,128)} %tk.1) | copy-start | bytes 1572868
  2.4 0.9 copy-start.1
  3.3 0.8 copy-start.2

commit v2 on v1

--- a/solution.py
+++ b/solution.py
@@ -14,9 +14,10 @@
 ROWS, COLS, FEAT = 256, 128, 64
 DEPTH = 384
 CHUNKS = 4
-NSEM = 192
+NSEM = 256
 UNIT = math.sqrt(3.0) * math.log2(math.e)
 LN2 = math.log(2.0)
+PLACE = (0, 1, 3, 2)
 
 
 def split2(x):
@@ -29,8 +30,9 @@
 
 
 def kernel(
-    tgt, feat, isc, noise_ref, tk, bm, sol, res,
-    zg, wy, fy, fx, fl, fr, kc, wb, vb, tn, p, rel, fin, nz, mk,
+    tgt_hbm, feat_hbm, isc_hbm, noise_hbm, tk_hbm, bm_hbm, sol, res,
+    tgt, feat, isc, noise_ref, tk, bm, ins,
+    zg, gx, wy, fy, fx, fl, fr, kc, wb, vb, tn, p, rel, fin, nz, mk,
     arsrc, arp, arz, ss, rs, ars, arr,
 ):
     me, z = lax.axis_index("cfg"), lax.axis_index("tm")
@@ -60,18 +62,26 @@
         copies.append(d)
         return d
 
+    pairs = ((bm_hbm, bm), (tgt_hbm, tgt), (isc_hbm, isc), (feat_hbm, feat), (noise_hbm, noise_ref), (tk_hbm, tk))
+    loads = [pltpu.make_async_copy(a, b, ins.at[i]) for i, (a, b) in enumerate(pairs)]
+    for d in loads:
+        d.start()
     barrier = pltpu.get_barrier_semaphore()
-    for dev in plane + column:
+    near = [mate, right, left, up, down, zup, zdown]
+    for dev in near:
         pl.semaphore_signal(barrier, inc=1, device_id=dev, device_id_type=MESH)
 
+    for d in loads[:4]:
+        d.wait()
     mk[...] = jnp.broadcast_to(bm[...].astype(F32), (COLS, ROWS)).T
-    nz[...] = jnp.broadcast_to(noise_ref[...], (COLS, ROWS)).T
-    zg[0, 0] = mk[...] * tgt[...]
+    r0 = mk[...] * tgt[...]
+    zg[0, 0] = r0
+    gx[0, 0] = r0
     fscaled = feat[...] * (isc[...].T * UNIT)
     fy[0, 0] = fscaled
     fx[0] = fscaled
 
-    pl.semaphore_wait(barrier, len(plane) + len(column))
+    pl.semaphore_wait(barrier, len(near))
 
     def ring4(buf, nh, fwd, back):
         d = {}
@@ -92,24 +102,32 @@
                 d["m", k, h] = copy(buf(0, k, h), buf(1, k, h), mate)
         return d
 
+    def order(nh):
+        return [(h, (h + nh // 2) % nh) for h in range(nh)]
+
+    def ring_start(d, nh):
+        for h, g in order(nh):
+            d["R1", h].start()
+            d["L1", g].start()
+
     def ring_step1(d, nh, mated):
-        for h in range(nh):
+        for h, g in order(nh):
             d["R1", h].wait_recv()
             if h < nh // 2:
                 d["2", h].start()
+            d["L1", g].wait_recv()
+            if g >= nh // 2:
+                d["2", g].start()
             if mated:
                 d["m", 1, h].start()
-            d["L1", h].wait_recv()
-            if h >= nh // 2:
-                d["2", h].start()
-            if mated:
-                d["m", 3, h].start()
+                d["m", 3, g].start()
 
     def ring_step2(d, nh, mated):
-        for h in range(nh):
-            d["2", h].wait_recv()
-            if mated:
-                d["m", 2, h].start()
+        for h, g in order(nh)[: nh // 2]:
+            for e in (h, g):
+                d["2", e].wait_recv()
+                if mated:
+                    d["m", 2, e].start()
 
     def mate_wait(d, nh, k):
         for h in range(nh):
@@ -130,15 +148,20 @@
 
     def z_start(d, c):
         d["R", 1, c].start()
-        d["L", 1, c].start()
-
-    def z_step(d, s):
-        for c in range(CHUNKS):
-            for way in "RL":
-                if (way, s, c) in d:
-                    d[way, s, c].wait_recv()
-                if (way, s + 1, c) in d:
-                    d[way, s + 1, c].start()
+        d["L", 1, (c + CHUNKS // 2) % CHUNKS].start()
+
+    def z_events(d):
+        for s in range(1, 5):
+            for c in range(CHUNKS if s < 4 else CHUNKS // 2):
+                for way, e in (("R", c), ("L", (c + CHUNKS // 2) % CHUNKS)):
+                    d[way, s, e].wait_recv()
+                    if (way, s + 1, e) in d:
+                        d[way, s + 1, e].start()
+                yield
+
+    def pump(events, n):
+        for _ in range(n):
+            next(events)
 
     def plane_copies(n):
         return [
@@ -189,12 +212,14 @@
     FH = ROWS // 2
     dfx = ring4(lambda k, h: fx.at[k, :, pl.ds(h * FH, FH)], 2, right, left)
     dfy = y_ring(lambda c, k, h: fy.at[c, k, :, pl.ds(h * FH, FH)], 2)
+    ring_start(dfy, 2)
+    ring_start(dfx, 2)
     for h in range(2):
-        for way in ("R1", "L1"):
-            dfy[way, h].start()
-            dfx[way, h].start()
         dfy["m", 0, h].start()
 
+    loads[4].wait()
+    nz[...] = jnp.broadcast_to(noise_ref[...], (COLS, ROWS)).T
+    loads[5].wait()
     for k in range(NZ):
         o = lax.rem(z + NZ - k, NZ)
         hi, lo = split2(tk[:, pl.ds(pl.multiple_of(o * COLS, COLS), COLS)])
@@ -222,7 +247,8 @@
     def build_left(k):
         hi, lo, n = parts(fx[k])
         stack = jnp.concatenate([-2.0 * hi, -2.0 * hi, -2.0 * lo, -2.0 * lo, place(n, 0)], axis=0)
-        fl[k * ROWS : (k + 1) * ROWS, :] = stack.T.astype(BF16)
+        i = PLACE[k]
+        fl[i * ROWS : (i + 1) * ROWS, :] = stack.T.astype(BF16)
 
     def build_right(c, k):
         hi, lo, n = parts(fy[c, k])
@@ -230,8 +256,7 @@
         j = c * NY + k
         fr[:, j * ROWS : (j + 1) * ROWS] = stack.astype(BF16)
 
-    def make_kernel(c, k):
-        build_right(c, k)
+    def make_kernel(c, k, first, end):
         j = c * NY + k
         cols = slice(j * ROWS, (j + 1) * ROWS)
         low = slice((8 + j) * ROWS, (9 + j) * ROWS)
@@ -247,7 +272,7 @@
             kc[sl, low] = lo
             return carry
 
-        lax.fori_loop(0, NX, one, 0)
+        lax.fori_loop(first, end, one, 0)
 
     def split_field(k, block):
         hi, lo = split2(block)
@@ -266,114 +291,167 @@
         wb[j * ROWS : (j + 1) * ROWS, :COLS] = hi
         wb[j * ROWS : (j + 1) * ROWS, COLS:] = lo
 
-    def apply_rows(it, k):
-        half = 8 * ROWS
-        sl = slice(k * ROWS, (k + 1) * ROWS)
-        acc = jnp.dot(kc[sl, :half], wb[...], preferred_element_type=F32)
-        acc += jnp.dot(kc[sl, half:], wb[...], preferred_element_type=F32)
-        p[it, k] = acc[:, :COLS] + acc[:, COLS:]
+    def apply_rows(it, k, early):
+        n = ROWS
+        sl = slice(PLACE[k] * n, (PLACE[k] + 1) * n)
+        acc = None
+        for lo, hi in ((0, 2), (3, 6), (7, 8)) if early else ((2, 3), (6, 7)):
+            for off in (0, 8):
+                part = jnp.dot(kc[sl, (off + lo) * n : (off + hi) * n], wb[lo * n : hi * n, :], preferred_element_type=F32)
+                acc = part if acc is None else acc + part
+        out = acc[:, :COLS] + acc[:, COLS:]
+        if early:
+            p[it, k] = out
+        else:
+            p[it, k] += out
 
     HR = ROWS // 2
     A, B = pl.ds(0, HR), pl.ds(HR, HR)
 
-    def spread(it):
-        relay_r = copy(p.at[it, 2, A], rel.at[it, 0], right)
-        relay_l = copy(p.at[it, 2, B], rel.at[it, 1], left)
-        own_r = copy(p.at[it, 3, B], fin.at[it, 0, B], right)
-        own_l = copy(p.at[it, 1, A], fin.at[it, 1, A], left)
-        sum_r = copy(p.at[it, 3, A], fin.at[it, 0, A], right)
-        sum_l = copy(p.at[it, 1, B], fin.at[it, 1, B], left)
-        apply_rows(it, 2)
-        relay_r.start()
-        relay_l.start()
-        apply_rows(it, 3)
-        own_r.start()
-        apply_rows(it, 1)
-        own_l.start()
-        relay_r.wait_recv()
-        p[it, 3, A] += rel[it, 0]
-        sum_r.start()
-        relay_l.wait_recv()
-        p[it, 1, B] += rel[it, 1]
-        sum_l.start()
-        apply_rows(it, 0)
-        own_r.wait_recv()
-        own_l.wait_recv()
-        sum_r.wait_recv()
-        sum_l.wait_recv()
-        return p[it, 0] + fin[it, 0] + fin[it, 1]
-
+    def spread(it, last):
+        half = CHUNKS // 2
+        sl = [pl.ds(c * CR, CR) for c in range(CHUNKS)]
+        d = {}
+        for c in range(CHUNKS):
+            if c < half:
+                d["relay", c] = copy(p.at[it, 2, sl[c]], rel.at[it, 0, sl[c]], right)
+                d["own", c] = copy(p.at[it, 1, sl[c]], fin.at[it, 1, sl[c]], left)
+                d["sum", c] = copy(p.at[it, 3, sl[c]], fin.at[it, 0, sl[c]], right)
+            else:
+                d["relay", c] = copy(p.at[it, 2, sl[c]], rel.at[it, 0, sl[c]], left)
+                d["own", c] = copy(p.at[it, 3, sl[c]], fin.at[it, 0, sl[c]], right)
+                d["sum", c] = copy(p.at[it, 1, sl[c]], fin.at[it, 1, sl[c]], left)
+        turns = [e for c in range(half) for e in (c, c + half)]
+        apply_rows(it, 2, False)
+        if last is not None:
+            apply_rows(it, 3, False)
+            apply_rows(it, 1, False)
+            apply_rows(it, 0, False)
+            last()
+        for c in turns:
+            d["relay", c].start()
+        if last is None:
+            apply_rows(it, 3, False)
+            apply_rows(it, 1, False)
+        for c in turns:
+            d["own", c].start()
+        if last is None:
+            apply_rows(it, 0, False)
+        for c in turns:
+            d["relay", c].wait_recv()
+            k = 3 if c < half else 1
+            p[it, k, sl[c]] += rel[it, 0, sl[c]]
+            d["sum", c].start()
+        for c in turns:
+            d["own", c].wait_recv()
+            d["sum", c].wait_recv()
+            yield sl[c], p[it, 0, sl[c]] + fin[it, 0, sl[c]] + fin[it, 1, sl[c]]
+
+    def x_ring(i):
+        return ring4(lambda k, h: gx.at[i, k, pl.ds(h * HR, HR)], 2, right, left)
+
+    def send_w(it):
+        d = y_ring(lambda c, k, h: wy.at[it, c, k, pl.ds(h * CR, CR)], CHUNKS)
+        for h in range(2):
+            wy[it, 0, 0, h * HR : (h + 1) * HR] = timed(h)
+        ring_start(d, CHUNKS)
+        for h in range(CHUNKS):
+            d["m", 0, h].start()
+        return d
+
+
+    def finish_w(it, d, stepped):
+        split_w(it, 0, 0)
+        mate_wait(d, CHUNKS, 0)
+        split_w(it, 1, 0)
+        if not stepped:
+            ring_step1(d, CHUNKS, True)
+        split_w(it, 0, 1)
+        split_w(it, 0, 3)
+        for k in (1, 3):
+            mate_wait(d, CHUNKS, k)
+            split_w(it, 1, k)
+        for k in (2, 3, 1, 0):
+            apply_rows(it, k, True)
+        ring_step2(d, CHUNKS, True)
+        split_w(it, 0, 2)
+        mate_wait(d, CHUNKS, 2)
+        split_w(it, 1, 2)
+
+    ev = z_events(dz)
     split_field(0, zg[0, 0])
+    build_left(0)
+    build_right(0, 0)
     ring_step1(dfx, 2, False)
     ring_step1(dfy, 2, True)
-    build_left(0)
-    z_step(dz, 1)
+    pump(ev, 1)
+    build_left(1)
+    build_left(3)
+    make_kernel(0, 0, 0, 3)
+    pump(ev, 1)
+    mate_wait(dfy, 2, 0)
+    build_right(1, 0)
+    make_kernel(1, 0, 0, 3)
+    pump(ev, 1)
+    build_right(0, 1)
+    make_kernel(0, 1, 0, 3)
+    pump(ev, 1)
     ring_step2(dfx, 2, False)
     ring_step2(dfy, 2, True)
-    for k in (1, 3, 2):
-        build_left(k)
+    dx = x_ring(0)
+    ring_start(dx, 2)
+    build_left(2)
     split_field(1, zg[0, 1])
     split_field(7, zg[0, 7])
-    make_kernel(0, 0)
-    make_kernel(0, 1)
-    z_step(dz, 2)
+    build_right(0, 3)
+    make_kernel(0, 3, 0, 4)
+    pump(ev, 1)
+    make_kernel(0, 0, 3, 4)
+    make_kernel(1, 0, 3, 4)
+    make_kernel(0, 1, 3, 4)
+    pump(ev, 1)
+    build_right(0, 2)
+    make_kernel(0, 2, 0, 4)
+    pump(ev, 2)
     split_field(2, zg[0, 2])
     split_field(6, zg[0, 6])
-    make_kernel(0, 3)
-    make_kernel(0, 2)
-    z_step(dz, 3)
+    mate_wait(dfy, 2, 1)
+    build_right(1, 1)
+    make_kernel(1, 1, 0, 4)
+    pump(ev, 1)
+    ring_step1(dx, 2, False)
+    mate_wait(dfy, 2, 3)
+    build_right(1, 3)
+    make_kernel(1, 3, 0, 4)
+    pump(ev, 1)
+    mate_wait(dfy, 2, 2)
+    build_right(1, 2)
+    make_kernel(1, 2, 0, 4)
+    pump(ev, 2)
+    ring_step2(dx, 2, False)
     split_field(3, zg[0, 3])
     split_field(5, zg[0, 5])
-    mate_wait(dfy, 2, 0)
-    make_kernel(1, 0)
-    mate_wait(dfy, 2, 1)
-    make_kernel(1, 1)
-    z_step(dz, 4)
+    pump(ev, 2)
     split_field(4, zg[0, 4])
-
-    def send_w(it):
-        d = y_ring(lambda c, k, h: wy.at[it, c, k, pl.ds(h * HR, HR)], 2)
-        for h in range(2):
-            wy[it, 0, 0, h * HR : (h + 1) * HR] = timed(h)
-            d["R1", h].start()
-            d["L1", h].start()
-            d["m", 0, h].start()
-        return d
-
     dw = send_w(0)
-    mate_wait(dfy, 2, 3)
-    make_kernel(1, 3)
-    ring_step1(dw, 2, True)
-    mate_wait(dfy, 2, 2)
-    make_kernel(1, 2)
-
-    def finish_w(it, d, stepped):
-        split_w(it, 0, 0)
-        if not stepped:
-            ring_step1(d, 2, True)
-        split_w(it, 0, 1)
-        split_w(it, 0, 3)
-        mate_wait(d, 2, 0)
-        split_w(it, 1, 0)
-        ring_step2(d, 2, True)
-        split_w(it, 0, 2)
-        for k in (1, 3, 2):
-            mate_wait(d, 2, k)
-            split_w(it, 1, k)
-
-    finish_w(0, dw, True)
-    total = spread(0)
-    r0 = zg[0, 0]
-    q = mk[...] * total + nz[...] * r0
-    zg[1, 0] = q
+    finish_w(0, dw, False)
 
     dz = z_ring(1)
-    for c in range(CHUNKS):
-        z_start(dz, c)
+    for i, (sl, total) in enumerate(spread(0, None)):
+        q = mk[sl, :] * total + nz[sl, :] * gx[0, 0, sl]
+        zg[1, 0, sl] = q
+        gx[1, 0, sl] = q
+        c = (i % 2) * CHUNKS // 2 + i // 2
+        for way in "RL" if i % 2 == 0 else "LR":
+            dz[way, 1, c].start()
+    r0, q = zg[0, 0], zg[1, 0]
     sum_start(0, r0 * r0, r0 * q)
-    z_step(dz, 1)
+    dx = x_ring(1)
+    ring_start(dx, 2)
+    ev = z_events(dz)
+    pump(ev, 3)
     sum_middle(0)
-    z_step(dz, 2)
+    pump(ev, 5)
     norm0, curv0 = sum_end(0)
     alpha = norm0 / curv0
 
@@ -381,34 +459,42 @@
         return zg[0, k] - alpha * zg[1, k]
 
     r1 = residual_block(0)
-    res[...] = r1
     sum_start(1, r1 * r1, r1)
+    ring_step1(dx, 2, False)
     split_field(0, r1)
     for k in (1, 7, 2, 6):
         split_field(k, residual_block(k))
-    z_step(dz, 3)
+    pump(ev, 4)
     for k in (3, 5):
         split_field(k, residual_block(k))
-    sum_middle(1)
-    z_step(dz, 4)
+    pump(ev, 2)
     split_field(4, residual_block(4))
     dw = send_w(1)
+    sum_middle(1)
+    ring_step2(dx, 2, False)
+    finish_w(1, dw, False)
     norm1, _ = sum_end(1)
-    finish_w(1, dw, False)
-    total = spread(1)
-
     beta = norm1 / norm0
-    r1 = res[...]
-    d1 = r1 + beta * zg[0, 0]
-    image = mk[...] * total + nz[...] * r1 + beta * zg[1, 0]
-    sum_start(2, d1 * image, d1)
-    p[1, 0] = d1
-    p[0, 0] = image
-    sum_middle(2)
+
+    def curvature():
+        r1 = gx[0, 0] - alpha * gx[1, 0]
+        d1 = r1 + beta * gx[0, 0]
+        terms = d1 * (p[1, 0] + nz[...] * r1 + beta * gx[1, 0])
+        for k in (1, 2, 3):
+            terms += p[1, k] * (gx[0, k] - alpha * gx[1, k] + beta * gx[0, k])
+        sum_start(2, terms, terms)
+
+    for i, (sl, total) in enumerate(spread(1, curvature)):
+        if i == 0:
+            sum_middle(2)
+        r1 = gx[0, 0, sl] - alpha * gx[1, 0, sl]
+        res[sl, :] = mk[sl, :] * total + nz[sl, :] * r1 + beta * gx[1, 0, sl]
     curv1, _ = sum_end(2)
     alpha1 = norm1 / curv1
-    sol[...] = alpha * zg[0, 0] + alpha1 * p[1, 0]
-    res[...] = res[...] - alpha1 * p[0, 0]
+    r0 = gx[0, 0]
+    r1 = r0 - alpha * gx[1, 0]
+    sol[...] = alpha * r0 + alpha1 * (r1 + beta * r0)
+    res[...] = r1 - alpha1 * res[...]
 
     for d in copies:
         d.wait_send()
@@ -423,10 +509,18 @@
     return pl.pallas_call(
         kernel,
         out_shape=(block, block),
-        in_specs=[vmem] * 6,
+        in_specs=[pl.BlockSpec(memory_space=pl.ANY)] * 6,
         out_specs=(vmem, vmem),
         scratch_shapes=[
+            pltpu.VMEM((ROWS, COLS), F32),
+            pltpu.VMEM((FEAT, ROWS), F32),
+            pltpu.VMEM((1, FEAT), F32),
+            pltpu.VMEM((1, ROWS), F32),
+            pltpu.VMEM((COLS, NZ * COLS), F32),
+            pltpu.VMEM((1, ROWS), jnp.int32),
+            pltpu.SemaphoreType.DMA((6,)),
             pltpu.VMEM((2, NZ, ROWS, COLS), F32),
+            pltpu.VMEM((2, NX, ROWS, COLS), F32),
             pltpu.VMEM((2, NCORE, NY, ROWS, COLS), F32),
             pltpu.VMEM((NCORE, NY, FEAT, ROWS), F32),
             pltpu.VMEM((NX, FEAT, ROWS), F32),
@@ -437,7 +531,7 @@
             pltpu.VMEM((ROWS, 2 * NZ * COLS), BF16),
             pltpu.VMEM((2 * COLS, NZ * COLS), BF16),
             pltpu.VMEM((2, NX, ROWS, COLS), F32),
-            pltpu.VMEM((2, 2, ROWS // 2, COLS), F32),
+            pltpu.VMEM((2, 1, ROWS, COLS), F32),
             pltpu.VMEM((2, 2, ROWS, COLS), F32),
             pltpu.VMEM((ROWS, COLS), F32),
             pltpu.VMEM((ROWS, COLS), F32),
@@ -450,7 +544,7 @@
             pltpu.SemaphoreType.DMA((3, 2)),
         ],
         compiler_params=pltpu.CompilerParams(
-            collective_id=0, has_side_effects=True, vmem_limit_bytes=40 * 1024 * 1024
+            collective_id=0, has_side_effects=True, vmem_limit_bytes=67043328
         ),
     )(
         targets, features.T, inv_scales.reshape(1, FEAT), noise.reshape(1, ROWS), time_kernel, block_mask.T

time: 102 us -> 88.1 us (0.86)
  Pallas kernels: 96.2 us -> 84.3 us
  local copies, waits for them, and re-layouts: 4.77 us -> 2.26 us
    pallas_call x1, Pallas kernels: 96.2 us -> 84.3 us  [body(): pl.pallas_call(kernel, out_shape=(block, block), in_specs=[pl.BlockSpec(m...]
    unnamed x14 -> x4, local copies, waits for them, and re-layouts: 4.77 us -> 2.26 us
where the time goes in v2:
time: 88.1 us; the launch traced here: 87.2 us
  Pallas kernels  84.3 us (96%)
  local copies, waits for them, and re-layouts  2.26 us (3%)
    pallas_call x1, Pallas kernels, body(): pl.pallas_call(kernel, out_shape=(block, block), in_specs=[pl.BlockSpec(m...  84.3 us
    unnamed x4, local copies, waits for them, and re-layouts  2.26 us

profile of v2, /device:TPU:1, one launch (start us, length us, event | category | flops | bytes accessed | tf_op | source)
XLA Modules:
  0.0 87.2 jit_solution(3143892666454187537)
XLA Ops:
  0.6 84.3 %shard_map.77 = (f32[256,128]{1,0:T(8,128)}, f32[256,128]{1,0:T(8,128)}) custom-call(f32[256,128]{1,0:T(8,128)} %tgt_hbm.1, f32[64,256]{1,0:T(8,128)} %bitcast.4, f32[1,64]{1,0:T(1,128)} %bitcast.7, f32[1,256]{1,0:T(1,128)} %bitcast.5, f32[128,1024]{1,0:T(8,128)} %tk_hbm.1, s32[1,256]{1,0:T(1,128)} %bitcast.6), custom_call_target="tpu_custom_call" | custom-call | tf_op jit(solution)/shard_map/pallas_call | solution.py:509
  84.9 0.0 copy-start
  85.0 1.6 %copy.10 = f32[256,128]{1,0:T(8,128)} copy(f32[256,128]{1,0:T(8,128)} %get-tuple-element.4) | data formatting | bytes 262144
  86.6 0.0 copy-done
  86.6 0.7 copy.11
Async XLA Ops:
  84.9 1.6 %copy-start = (f32[256,128]{1,0:T(8,128)S(1)}, f32[256,128]{1,0:T(8,128)}, u32[]{:S(2)}) copy-start(f32[256,128]{1,0:T(8,128)} %get-tuple-element.5) | copy-start | bytes 393220

commit v3 on v2

--- a/solution.py
+++ b/solution.py
@@ -261,8 +261,8 @@
         cols = slice(j * ROWS, (j + 1) * ROWS)
         low = slice((8 + j) * ROWS, (9 + j) * ROWS)
 
-        def one(i, carry):
-            sl = pl.ds(pl.multiple_of(i * ROWS, ROWS), ROWS)
+        def one(i):
+            sl = slice(i * ROWS, (i + 1) * ROWS)
             d2 = jnp.dot(fl[sl, :], fr[:, cols], preferred_element_type=F32)
             d2 = jnp.maximum(d2, 1e-30)
             u = d2 * lax.rsqrt(d2)
@@ -270,20 +270,25 @@
             hi, lo = split2(value)
             kc[sl, cols] = hi
             kc[sl, low] = lo
-            return carry
-
-        lax.fori_loop(first, end, one, 0)
+
+        for i in range(first, end):
+            one(i)
 
     def split_field(k, block):
         hi, lo = split2(block)
         vb[:, k * COLS : (k + 1) * COLS] = hi
         vb[:, (NZ + k) * COLS : (NZ + k + 1) * COLS] = lo
 
-    def timed(c):
-        sl = slice(c * ROWS // 2, (c + 1) * ROWS // 2)
-        half = NZ * COLS
-        acc = nt_dot(vb[sl, :half], tn[...]) + nt_dot(vb[sl, half:], tn[...])
+    def timed(spans):
+        acc = None
+        for off in (0, NZ):
+            for lo, hi in spans:
+                part = nt_dot(vb[:, (off + lo) * COLS : (off + hi) * COLS], tn[:, lo * COLS : hi * COLS])
+                acc = part if acc is None else acc + part
         return acc[:, :COLS] + acc[:, COLS:]
+
+    def timed_early(it):
+        wy[it, 0, 0] = timed(((0, 4), (5, 8)))
 
     def split_w(it, c, k):
         hi, lo = split2(wy[it, c, k])
@@ -342,6 +347,8 @@
             k = 3 if c < half else 1
             p[it, k, sl[c]] += rel[it, 0, sl[c]]
             d["sum", c].start()
+        if last is not None:
+            sum_middle(2)
         for c in turns:
             d["own", c].wait_recv()
             d["sum", c].wait_recv()
@@ -352,8 +359,7 @@
 
     def send_w(it):
         d = y_ring(lambda c, k, h: wy.at[it, c, k, pl.ds(h * CR, CR)], CHUNKS)
-        for h in range(2):
-            wy[it, 0, 0, h * HR : (h + 1) * HR] = timed(h)
+        wy[it, 0, 0] += timed(((4, 5),))
         ring_start(d, CHUNKS)
         for h in range(CHUNKS):
             d["m", 0, h].start()
@@ -431,6 +437,7 @@
     ring_step2(dx, 2, False)
     split_field(3, zg[0, 3])
     split_field(5, zg[0, 5])
+    timed_early(0)
     pump(ev, 2)
     split_field(4, zg[0, 4])
     dw = send_w(0)
@@ -442,8 +449,10 @@
         zg[1, 0, sl] = q
         gx[1, 0, sl] = q
         c = (i % 2) * CHUNKS // 2 + i // 2
-        for way in "RL" if i % 2 == 0 else "LR":
-            dz[way, 1, c].start()
+        dz["RL"[i % 2], 1, c].start()
+    for c in range(CHUNKS // 2):
+        dz["R", 1, c + CHUNKS // 2].start()
+        dz["L", 1, c].start()
     r0, q = zg[0, 0], zg[1, 0]
     sum_start(0, r0 * r0, r0 * q)
     dx = x_ring(1)
@@ -451,7 +460,8 @@
     ev = z_events(dz)
     pump(ev, 3)
     sum_middle(0)
-    pump(ev, 5)
+    pump(ev, 7)
+    ring_step1(dx, 2, False)
     norm0, curv0 = sum_end(0)
     alpha = norm0 / curv0
 
@@ -460,13 +470,13 @@
 
     r1 = residual_block(0)
     sum_start(1, r1 * r1, r1)
-    ring_step1(dx, 2, False)
     split_field(0, r1)
     for k in (1, 7, 2, 6):
         split_field(k, residual_block(k))
-    pump(ev, 4)
+    pump(ev, 2)
     for k in (3, 5):
         split_field(k, residual_block(k))
+    timed_early(1)
     pump(ev, 2)
     split_field(4, residual_block(4))
     dw = send_w(1)
@@ -484,9 +494,7 @@
             terms += p[1, k] * (gx[0, k] - alpha * gx[1, k] + beta * gx[0, k])
         sum_start(2, terms, terms)
 
-    for i, (sl, total) in enumerate(spread(1, curvature)):
-        if i == 0:
-            sum_middle(2)
+    for sl, total in spread(1, curvature):
         r1 = gx[0, 0, sl] - alpha * gx[1, 0, sl]
         res[sl, :] = mk[sl, :] * total + nz[sl, :] * r1 + beta * gx[1, 0, sl]
     curv1, _ = sum_end(2)

time: 88.1 us -> 84 us (0.953)
  Pallas kernels: 84.3 us -> 81 us
    pallas_call x1, Pallas kernels: 84.3 us -> 81 us  [body(): pl.pallas_call(kernel, out_shape=(block, block), in_specs=[pl.BlockSpec(m...]
where the time goes in v3:
time: 84 us; the launch traced here: 83.9 us
  Pallas kernels  81 us (96%)
  local copies, waits for them, and re-layouts  2.26 us (3%)
    pallas_call x1, Pallas kernels, body(): pl.pallas_call(kernel, out_shape=(block, block), in_specs=[pl.BlockSpec(m...  81 us
    unnamed x4, local copies, waits for them, and re-layouts  2.26 us

profile of v3, /device:TPU:1, one launch (start us, length us, event | category | flops | bytes accessed | tf_op | source)
XLA Modules:
  0.0 83.9 jit_solution(3760025262865118239)
XLA Ops:
  0.6 81.0 %shard_map.77 = (f32[256,128]{1,0:T(8,128)}, f32[256,128]{1,0:T(8,128)}) custom-call(f32[256,128]{1,0:T(8,128)} %tgt_hbm.1, f32[64,256]{1,0:T(8,128)} %bitcast.4, f32[1,64]{1,0:T(1,128)} %bitcast.7, f32[1,256]{1,0:T(1,128)} %bitcast.5, f32[128,1024]{1,0:T(8,128)} %tk_hbm.1, s32[1,256]{1,0:T(1,128)} %bitcast.6), custom_call_target="tpu_custom_call" | custom-call | tf_op jit(solution)/shard_map/pallas_call | solution.py:517
  81.7 0.0 copy-start
  81.7 1.6 %copy.10 = f32[256,128]{1,0:T(8,128)} copy(f32[256,128]{1,0:T(8,128)} %get-tuple-element.4) | data formatting | bytes 262144
  83.3 0.0 copy-done
  83.3 0.7 copy.11
Async XLA Ops:
  81.7 1.6 %copy-start = (f32[256,128]{1,0:T(8,128)S(1)}, f32[256,128]{1,0:T(8,128)}, u32[]{:S(2)}) copy-start(f32[256,128]{1,0:T(8,128)} %get-tuple-element.5) | copy-start | bytes 393220

commit v4 on v3

--- a/solution.py
+++ b/solution.py
@@ -313,11 +313,11 @@
     HR = ROWS // 2
     A, B = pl.ds(0, HR), pl.ds(HR, HR)
 
-    def spread(it, last):
-        half = CHUNKS // 2
-        sl = [pl.ds(c * CR, CR) for c in range(CHUNKS)]
+    def spread(it, last, nc):
+        half, size = nc // 2, ROWS // nc
+        sl = [pl.ds(c * size, size) for c in range(nc)]
         d = {}
-        for c in range(CHUNKS):
+        for c in range(nc):
             if c < half:
                 d["relay", c] = copy(p.at[it, 2, sl[c]], rel.at[it, 0, sl[c]], right)
                 d["own", c] = copy(p.at[it, 1, sl[c]], fin.at[it, 1, sl[c]], left)
@@ -358,30 +358,30 @@
         return ring4(lambda k, h: gx.at[i, k, pl.ds(h * HR, HR)], 2, right, left)
 
     def send_w(it):
-        d = y_ring(lambda c, k, h: wy.at[it, c, k, pl.ds(h * CR, CR)], CHUNKS)
+        d = y_ring(lambda c, k, h: wy.at[it, c, k, pl.ds(h * HR, HR)], 2)
         wy[it, 0, 0] += timed(((4, 5),))
-        ring_start(d, CHUNKS)
-        for h in range(CHUNKS):
+        ring_start(d, 2)
+        for h in range(2):
             d["m", 0, h].start()
         return d
 
 
     def finish_w(it, d, stepped):
         split_w(it, 0, 0)
-        mate_wait(d, CHUNKS, 0)
+        mate_wait(d, 2, 0)
         split_w(it, 1, 0)
         if not stepped:
-            ring_step1(d, CHUNKS, True)
+            ring_step1(d, 2, True)
         split_w(it, 0, 1)
         split_w(it, 0, 3)
         for k in (1, 3):
-            mate_wait(d, CHUNKS, k)
+            mate_wait(d, 2, k)
             split_w(it, 1, k)
         for k in (2, 3, 1, 0):
             apply_rows(it, k, True)
-        ring_step2(d, CHUNKS, True)
+        ring_step2(d, 2, True)
         split_w(it, 0, 2)
-        mate_wait(d, CHUNKS, 2)
+        mate_wait(d, 2, 2)
         split_w(it, 1, 2)
 
     ev = z_events(dz)
@@ -404,8 +404,6 @@
     pump(ev, 1)
     ring_step2(dfx, 2, False)
     ring_step2(dfy, 2, True)
-    dx = x_ring(0)
-    ring_start(dx, 2)
     build_left(2)
     split_field(1, zg[0, 1])
     split_field(7, zg[0, 7])
@@ -425,7 +423,6 @@
     build_right(1, 1)
     make_kernel(1, 1, 0, 4)
     pump(ev, 1)
-    ring_step1(dx, 2, False)
     mate_wait(dfy, 2, 3)
     build_right(1, 3)
     make_kernel(1, 3, 0, 4)
@@ -434,7 +431,6 @@
     build_right(1, 2)
     make_kernel(1, 2, 0, 4)
     pump(ev, 2)
-    ring_step2(dx, 2, False)
     split_field(3, zg[0, 3])
     split_field(5, zg[0, 5])
     timed_early(0)
@@ -444,7 +440,7 @@
     finish_w(0, dw, False)
 
     dz = z_ring(1)
-    for i, (sl, total) in enumerate(spread(0, None)):
+    for i, (sl, total) in enumerate(spread(0, None, CHUNKS)):
         q = mk[sl, :] * total + nz[sl, :] * gx[0, 0, sl]
         zg[1, 0, sl] = q
         gx[1, 0, sl] = q
@@ -455,13 +451,15 @@
         dz["L", 1, c].start()
     r0, q = zg[0, 0], zg[1, 0]
     sum_start(0, r0 * r0, r0 * q)
-    dx = x_ring(1)
+    dx, dx0 = x_ring(1), x_ring(0)
     ring_start(dx, 2)
+    ring_start(dx0, 2)
     ev = z_events(dz)
     pump(ev, 3)
     sum_middle(0)
     pump(ev, 7)
     ring_step1(dx, 2, False)
+    ring_step1(dx0, 2, False)
     norm0, curv0 = sum_end(0)
     alpha = norm0 / curv0
 
@@ -482,6 +480,7 @@
     dw = send_w(1)
     sum_middle(1)
     ring_step2(dx, 2, False)
+    ring_step2(dx0, 2, False)
     finish_w(1, dw, False)
     norm1, _ = sum_end(1)
     beta = norm1 / norm0
@@ -494,7 +493,7 @@
             terms += p[1, k] * (gx[0, k] - alpha * gx[1, k] + beta * gx[0, k])
         sum_start(2, terms, terms)
 
-    for sl, total in spread(1, curvature):
+    for sl, total in spread(1, curvature, 2):
         r1 = gx[0, 0, sl] - alpha * gx[1, 0, sl]
         res[sl, :] = mk[sl, :] * total + nz[sl, :] * r1 + beta * gx[1, 0, sl]
     curv1, _ = sum_end(2)

time: 84 us -> 82.6 us (0.983)
  Pallas kernels: 81 us -> 79.5 us
    pallas_call x1, Pallas kernels: 81 us -> 79.5 us  [body(): pl.pallas_call(kernel, out_shape=(block, block), in_specs=[pl.BlockSpec(m...]
where the time goes in v4:
time: 82.6 us; the launch traced here: 82.4 us
  Pallas kernels  79.5 us (96%)
  local copies, waits for them, and re-layouts  2.26 us (3%)
    pallas_call x1, Pallas kernels, body(): pl.pallas_call(kernel, out_shape=(block, block), in_specs=[pl.BlockSpec(m...  79.5 us
    unnamed x4, local copies, waits for them, and re-layouts  2.26 us

profile of v4, /device:TPU:1, one launch (start us, length us, event | category | flops | bytes accessed | tf_op | source)
XLA Modules:
  0.0 82.4 jit_solution(3024890283128646428)
XLA Ops:
  0.6 79.5 %shard_map.77 = (f32[256,128]{1,0:T(8,128)}, f32[256,128]{1,0:T(8,128)}) custom-call(f32[256,128]{1,0:T(8,128)} %tgt_hbm.1, f32[64,256]{1,0:T(8,128)} %bitcast.4, f32[1,64]{1,0:T(1,128)} %bitcast.7, f32[1,256]{1,0:T(1,128)} %bitcast.5, f32[128,1024]{1,0:T(8,128)} %tk_hbm.1, s32[1,256]{1,0:T(1,128)} %bitcast.6), custom_call_target="tpu_custom_call" | custom-call | tf_op jit(solution)/shard_map/pallas_call | solution.py:516
  80.2 0.0 copy-start
  80.2 1.6 %copy.10 = f32[256,128]{1,0:T(8,128)} copy(f32[256,128]{1,0:T(8,128)} %get-tuple-element.4) | data formatting | bytes 262144
  81.8 0.0 copy-done
  81.8 0.7 copy.11
Async XLA Ops:
  80.2 1.6 %copy-start = (f32[256,128]{1,0:T(8,128)S(1)}, f32[256,128]{1,0:T(8,128)}, u32[]{:S(2)}) copy-start(f32[256,128]{1,0:T(8,128)} %get-tuple-element.5) | copy-start | bytes 393220

commit v5 on v4

--- a/solution.py
+++ b/solution.py
@@ -95,9 +95,10 @@
                 d["2", h] = copy(buf(3, h), buf(2, h), back)
         return d
 
-    def y_ring(buf, nh):
+    def y_ring(buf, nh, own):
         d = ring4(lambda k, h: buf(0, k, h), nh, up, down)
-        for k in (0, 1, 3, 2):
+        d["m", 0, 0] = copy(*own, mate)
+        for k in (1, 3, 2):
             for h in range(nh):
                 d["m", k, h] = copy(buf(0, k, h), buf(1, k, h), mate)
         return d
@@ -130,7 +131,7 @@
                     d["m", 2, e].start()
 
     def mate_wait(d, nh, k):
-        for h in range(nh):
+        for h in range(nh if k else 1):
             d["m", k, h].wait_recv()
 
     CR = ROWS // CHUNKS
@@ -211,11 +212,10 @@
         z_start(dz, c)
     FH = ROWS // 2
     dfx = ring4(lambda k, h: fx.at[k, :, pl.ds(h * FH, FH)], 2, right, left)
-    dfy = y_ring(lambda c, k, h: fy.at[c, k, :, pl.ds(h * FH, FH)], 2)
+    dfy = y_ring(lambda c, k, h: fy.at[c, k, :, pl.ds(h * FH, FH)], 2, (fy.at[0, 0], fy.at[1, 0]))
     ring_start(dfy, 2)
     ring_start(dfx, 2)
-    for h in range(2):
-        dfy["m", 0, h].start()
+    dfy["m", 0, 0].start()
 
     loads[4].wait()
     nz[...] = jnp.broadcast_to(noise_ref[...], (COLS, ROWS)).T
@@ -358,11 +358,10 @@
         return ring4(lambda k, h: gx.at[i, k, pl.ds(h * HR, HR)], 2, right, left)
 
     def send_w(it):
-        d = y_ring(lambda c, k, h: wy.at[it, c, k, pl.ds(h * HR, HR)], 2)
+        d = y_ring(lambda c, k, h: wy.at[it, c, k, pl.ds(h * HR, HR)], 2, (wy.at[it, 0, 0], wy.at[it, 1, 0]))
         wy[it, 0, 0] += timed(((4, 5),))
         ring_start(d, 2)
-        for h in range(2):
-            d["m", 0, h].start()
+        d["m", 0, 0].start()
         return d
 
 

time: 82.6 us -> 82.5 us (level)
  no operation moved by 1% of the time
where the time goes in v5:
time: 82.5 us; the launch traced here: 82.4 us
  Pallas kernels  79.5 us (96%)
  local copies, waits for them, and re-layouts  2.26 us (3%)
    pallas_call x1, Pallas kernels, body(): pl.pallas_call(kernel, out_shape=(block, block), in_specs=[pl.BlockSpec(m...  79.5 us
    unnamed x4, local copies, waits for them, and re-layouts  2.26 us

profile of v5, /device:TPU:1, one launch (start us, length us, event | category | flops | bytes accessed | tf_op | source)
XLA Modules:
  0.0 82.4 jit_solution(6309163923578133555)
XLA Ops:
  0.6 79.5 %shard_map.77 = (f32[256,128]{1,0:T(8,128)}, f32[256,128]{1,0:T(8,128)}) custom-call(f32[256,128]{1,0:T(8,128)} %tgt_hbm.1, f32[64,256]{1,0:T(8,128)} %bitcast.4, f32[1,64]{1,0:T(1,128)} %bitcast.7, f32[1,256]{1,0:T(1,128)} %bitcast.5, f32[128,1024]{1,0:T(8,128)} %tk_hbm.1, s32[1,256]{1,0:T(1,128)} %bitcast.6), custom_call_target="tpu_custom_call" | custom-call | tf_op jit(solution)/shard_map/pallas_call | solution.py:515
  80.2 0.0 copy-start
  80.2 1.6 %copy.10 = f32[256,128]{1,0:T(8,128)} copy(f32[256,128]{1,0:T(8,128)} %get-tuple-element.4) | data formatting | bytes 262144
  81.8 0.0 copy-done
  81.8 0.7 copy.11
Async XLA Ops:
  80.2 1.6 %copy-start = (f32[256,128]{1,0:T(8,128)S(1)}, f32[256,128]{1,0:T(8,128)}, u32[]{:S(2)}) copy-start(f32[256,128]{1,0:T(8,128)} %get-tuple-element.5) | copy-start | bytes 393220
